TPU v7x, 32 devices: a whole 2x2x4 slice. The times are simulated.
32 devices in a mesh: beam: 4 (over x, core), det: 2 (over y), slab: 4 (over z).
Axes of the slice: x: 2, y: 2, z: 4, core: 2. Of those that a mesh axis runs over, the one named last changes fastest.
Arguments:
- concentration: float32 [4, 32, 1024, 256], P(None, 'slab', 'beam', 'det'), may hold values from 0.1 to 1
- cross_section: float32 [4, 16], replicated, may hold values from 0.2 to 2
- line_attenuation: float32 [4], replicated, may hold values from 0.5 to 2
- energy_index: int32 [4], replicated, may hold values from 0 to 15
- fan_offset: int32 [256], replicated, may hold values from 0 to 28
- fan_weight: int32 [256, 4], replicated, may hold values from 1 to 3
- measured: float32 [4, 256, 256], P(None, None, 'det'), may hold values from 0 to 6
Outputs:
- voxel_grad: float32 [4, 32, 1024, 256], P(None, 'slab', 'beam', 'det')
- residual: float32 [4, 256, 256], P(None, ('beam', 'slab'), 'det')
All inputs are finite; a program needn't handle non-finite values.
Results may differ from a plain program's by a relative error of at most 0.00013.
Values sent between devices are 32-bit elements; how exact they have to be, the bound alone decides.
No kernel may reach another device: no remote copies, remote signals or barrier semaphores. Data moves between devices by JAX's collectives and lax.ppermute only.
A program may use at most 128 MiB of HBM per device.

v0:
```python
import functools
import math

import jax
import jax.numpy as jnp
from jax import lax
from jax.experimental import pallas as pl
from jax.experimental.pallas import tpu as pltpu
from jax.sharding import PartitionSpec as P


VMEM, SMEM, HBM = pltpu.VMEM, pltpu.SMEM, pltpu.HBM
F32, BF16 = jnp.float32, jnp.bfloat16
LANES = 128
CHUNK = 32
STEP = 16
LN2 = math.log(2.0)
LOG2E = 1.0 / LN2


def call(body, out_shape, out_spaces, in_spaces, scratch=(), limit=8, cost=None, aliases=None):
    flops, exps, size = cost
    return pl.pallas_call(
        body,
        out_shape=out_shape,
        in_specs=[pl.BlockSpec(memory_space=s) for s in in_spaces],
        out_specs=[pl.BlockSpec(memory_space=s) for s in out_spaces],
        scratch_shapes=list(scratch),
        input_output_aliases=aliases or {},
        compiler_params=pltpu.CompilerParams(vmem_limit_bytes=limit << 20),
        cost_estimate=pl.CostEstimate(flops=flops, transcendentals=exps, bytes_accessed=size),
    )


def plain(*shape):
    return jax.ShapeDtypeStruct(shape, F32)


def split(value):
    high = value.astype(BF16)
    low = (value - high.astype(F32)).astype(BF16)
    return jnp.concatenate([high, low], axis=1)


def lane_sums(width, beyond):
    row = lax.broadcasted_iota(jnp.int32, (width, 2 * width), 0)
    col = lax.broadcasted_iota(jnp.int32, (width, 2 * width), 1)
    part = (row > col) if beyond else (row < col)
    ones = jnp.where(part | (col >= width), 1.0, 0.0).astype(BF16)
    return jnp.concatenate([ones, ones], axis=0)


def selected(cross_ref, index_ref):
    n_energy = index_ref.shape[0]
    columns = [index_ref[e] for e in range(n_energy)]
    return [[cross_ref[s, columns[e]] for e in range(n_energy)] for s in range(cross_ref.shape[0])]


def planes(plane_ref, n_species, n_energy):
    cross = [[plane_ref[s * n_energy + e] for e in range(n_energy)] for s in range(n_species)]
    return cross, [plane_ref[n_species * n_energy + s] for s in range(n_species)]


def weighted(weights, values):
    total = weights[0] * values[0]
    for weight, value in zip(weights[1:], values[1:]):
        total = total + weight * value
    return total


def load_body(
    scale, scale_x, line_hbm, cross_hbm, index_hbm, conc_hbm, conc_ref, emit_ref, beyond_ref, total_ref, plane_ref,
    line_ref, cross_ref, index_ref, small_sems, sems,
):
    n_species, depth, rows, width = conc_hbm.shape
    n_early = emit_ref.shape[0]
    ends = list(range(CHUNK, rows, CHUNK)) + [rows - CHUNK // 2, rows]
    starts = [0] + ends[:-1]

    def copies(chunk):
        span = pl.ds(starts[chunk], ends[chunk] - starts[chunk])
        return [
            pltpu.make_async_copy(conc_hbm.at[:, z, span, :], conc_ref.at[:, span, z, :], sems.at[chunk])
            for z in range(depth)
        ]

    small = [
        pltpu.make_async_copy(source, target, small_sems.at[i])
        for i, (source, target) in enumerate(
            [(line_hbm, line_ref), (cross_hbm, cross_ref), (index_hbm, index_ref)]
        )
    ]
    for copy in small:
        copy.start()
    for chunk in range(len(ends)):
        for copy in copies(chunk):
            copy.start()
    table = lane_sums(width, True)
    lane = lax.broadcasted_iota(jnp.int32, (depth, LANES), 1)
    for copy in small:
        copy.wait()
    line = [line_ref[s] * scale for s in range(n_species)]
    sigma = selected(cross_ref, index_ref)
    scalars = [v for row in sigma for v in row] + [line_ref[s] for s in range(n_species)]
    for i, value in enumerate(scalars):
        plane_ref[i] = jnp.full((depth, width), value)
    sigma = [[v * scale_x for v in row] for row in sigma]
    total = jnp.zeros((depth, LANES), F32)
    for chunk, (start, end) in enumerate(zip(starts, ends)):
        for copy in copies(chunk):
            copy.wait()
        absorber = []
        for x in range(start, end):
            conc = [conc_ref[s, x] for s in range(n_species)]
            absorber.append(weighted(line, conc))
            for e in range(n_early):
                emit_ref[e, x] = weighted([sigma[s][e] for s in range(n_species)], conc)
        sums = jnp.dot(split(jnp.concatenate(absorber, axis=0)), table, preferred_element_type=F32)
        for q, x in enumerate(range(start, end)):
            here = sums[q * depth : (q + 1) * depth]
            beyond_ref[x] = here[:, :width]
            total = jnp.where(lane == x % LANES, here[:, width : width + LANES], total)
        if end % LANES == 0:
            total_ref[:, end - LANES : end] = total


def local_body(scale, plane_ref, conc_ref, early_ref, beyond_ref, trans_ref, emit_ref, pair_ref):
    n_energy, rows, depth, width = trans_ref.shape
    n_species, n_early = conc_ref.shape[0], early_ref.shape[0]
    sigma = [[v * scale for v in row] for row in planes(plane_ref, n_species, n_energy)[0]]

    def step(block, carry):
        path, sums = list(carry[:n_energy]), list(carry[n_energy:])
        for q in range(STEP):
            x = block * STEP + q
            beyond = beyond_ref[x]
            conc = [conc_ref[s, x] for s in range(n_species)]
            for e in range(n_energy):
                if e < n_early:
                    emission = early_ref[e, x]
                else:
                    emission = weighted([sigma[s][e] for s in range(n_species)], conc)
                trans = jnp.exp2(path[e] + beyond)
                trans_ref[e, x] = trans
                emit = emission * trans
                emit_ref[e, x] = emit
                path[e] = path[e] + emission
                sums[e] = sums[e] + emit
        return tuple(path + sums)

    zero = jnp.zeros((depth, width), F32)
    carry = lax.fori_loop(0, rows // STEP, step, (zero,) * (2 * n_energy))
    for e in range(n_energy):
        pair_ref[0, e] = carry[e]
        pair_ref[1, e] = carry[n_energy + e]


def columns(source_ref, change, width):
    depth, rows = source_ref.shape
    for part in range(rows // LANES):
        held = change(source_ref[:, part * LANES : (part + 1) * LANES])
        for q in range(LANES):
            yield part * LANES + q, jnp.broadcast_to(held[:, q : q + 1], (depth, width))


def line_body(count, far_ref, emit_ref, local_ref, far_out, pair_ref):
    n_energy, _, _, width = emit_ref.shape
    last = lax.axis_index("det") == count - 1

    @pl.when(last)
    def _():
        pair_ref[...] = local_ref[...]

    @pl.when(jnp.logical_not(last))
    def _():
        sums = [[None, None] for _ in range(n_energy)]
        for x, factor in columns(far_ref, jnp.exp2, width):
            far_out[x] = factor
            for e in range(n_energy):
                value = factor * emit_ref[e, x]
                sums[e][x % 2] = value if x < 2 else sums[e][x % 2] + value
        for e in range(n_energy):
            pair_ref[0, e] = local_ref[0, e]
            pair_ref[1, e] = sums[e][0] + sums[e][1]


def merge_body(*refs):
    pairs, (total_ref, up_ref, further_ref) = refs[:-3], refs[-3:]
    beam = lax.axis_index("beam")
    state = [(ref[0], ref[1]) for ref in pairs]
    up, further = jnp.zeros_like(state[0][0]), jnp.zeros_like(state[0][0])
    distance = 1
    while len(state) > 1:
        lower = (beam & distance) == 0
        merged = []
        for i in range(0, len(state), 2):
            (span, sums), (other_span, other_sums) = state[i], state[i + 1]
            fade = jnp.exp2(jnp.where(lower, span, other_span))
            late = fade * jnp.where(lower, other_sums, sums)
            if i == 0:
                further = jnp.where(lower, further + late, fade * further)
                up = jnp.where(lower, up, up + other_span)
            merged.append((span + other_span, jnp.where(lower, sums, other_sums) + late))
        state = merged
        distance *= 2
    total_ref[0] = state[0][1]
    up_ref[...] = up
    further_ref[...] = further


def ahead_body(count, far_ref, trans_ref, emit_ref, fluor_ref, rest_ref):
    n_energy, rows, depth, width = emit_ref.shape

    last = lax.axis_index("det") == count - 1

    def step(block, ahead):
        ahead = list(ahead)
        for q in range(STEP):
            x = rows - 1 - (block * STEP + q)
            far = jnp.where(last, 1.0, far_ref[x])
            for e in range(n_energy):
                fluor = far * emit_ref[e, x]
                fluor_ref[e, x] = fluor
                rest_ref[e, x] = far * trans_ref[e, x] + ahead[e]
                ahead[e] = ahead[e] + LN2 * fluor
        return tuple(ahead)

    zero = jnp.zeros((depth, width), F32)
    lax.fori_loop(0, rows // STEP, step, (zero,) * n_energy)


def fan_body(scale, near_slabs, offset_ref, weight_ref, measured_ref, own_ref, gram_ref, pull_ref, turned_ref):
    depth, n_slab = gram_ref.shape[0], turned_ref.shape[1] // gram_ref.shape[0]
    taps, pixels = weight_ref.shape
    own = lax.axis_index("slab")
    offset = jnp.broadcast_to(offset_ref[...], (depth, pixels))
    level = lax.broadcasted_iota(jnp.int32, (depth, pixels), 0) - offset
    taps = [jnp.broadcast_to(weight_ref[j : j + 1, :], (depth, pixels)).astype(F32) for j in range(taps)]

    def block(slab):
        place = level + slab * depth
        found = jnp.zeros((depth, pixels), F32)
        for j, tap in enumerate(taps):
            found = found + jnp.where(place == j, tap, 0.0)
        return found

    blocks = [block(own ^ r) for r in range(n_slab)]
    turned_ref[...] = jnp.concatenate(blocks, axis=0).T
    odd = own + jnp.where((own & 1) == 1, 1, -1)
    near = jnp.concatenate([block(odd) if r is None else blocks[r] for r in near_slabs], axis=0)
    gram = lax.dot_general(
        blocks[0].astype(BF16), near.astype(BF16), (((1,), (1,)), ((), ())), preferred_element_type=F32
    )
    gram_ref[...] = gram
    n_energy, _, width = pull_ref.shape
    sums = weigh(gram, [(0, own_ref, 0)], depth, n_energy, width)
    for e in range(n_energy):
        pull_ref[e] = sums[e] * scale - jnp.dot(
            blocks[0], measured_ref[e], precision=lax.Precision.HIGHEST, preferred_element_type=F32
        )


def weigh(weights, lines, depth, n_energy, width):
    height = weights.shape[0]
    sums = [[None, None] for _ in range(n_energy)]
    for order, (r, lines_ref, i) in enumerate(lines):
        for z in range(depth):
            place = r * depth + z
            weight = jnp.broadcast_to(weights[:, place : place + 1], (height, width))
            for e in range(n_energy):
                value = weight * lines_ref[i, e, z : z + 1, :]
                sums[e][z % 2] = value if order == 0 and z < 2 else sums[e][z % 2] + value
    return [a + b for a, b in sums]


def back_body(scale, count, plane_ref, gram_ref, pull_ref, up_ref, further_ref, fluor_ref, *refs):
    lines, (near_ref, total_ref, gain_ref, shift_ref) = refs[:-4], refs[-4:]
    n_energy, _, depth, width = fluor_ref.shape
    n_species = shift_ref.shape[0]
    sums = weigh(gram_ref[...], [(r + 1, ref, 0) for r, ref in enumerate(lines)], depth, n_energy, width)
    back = [sums[e] * scale + pull_ref[e] for e in range(n_energy)]
    gain = [back[e] * jnp.exp2(up_ref[e]) for e in range(n_energy)]
    sigma, _ = planes(plane_ref, n_species, n_energy)
    pushed = [LN2 * back[e] * further_ref[e] for e in range(n_energy)]
    for e in range(n_energy):
        gain_ref[e] = gain[e]
    for s in range(n_species):
        shift_ref[s] = weighted(sigma[s], pushed)
    last = jnp.logical_and(lax.axis_index("det") == count - 1, count > 1)

    @pl.when(jnp.logical_not(last))
    def _():
        column_sums(gain, fluor_ref, near_ref, total_ref)

    @pl.when(last)
    def _():
        total_ref[...] = jnp.zeros_like(total_ref)


def column_sums(gain, fluor_ref, near_ref, total_ref):
    n_energy, rows, depth, width = fluor_ref.shape
    table = lane_sums(width, False)
    lane = lax.broadcasted_iota(jnp.int32, (depth, LANES), 1)
    total = jnp.zeros((depth, LANES), F32)
    for start in range(0, rows, CHUNK):
        span = range(start, start + CHUNK)
        heavy = [weighted(gain, [fluor_ref[e, x] for e in range(n_energy)]) for x in span]
        found = jnp.dot(split(jnp.concatenate(heavy, axis=0)), table, preferred_element_type=F32)
        for q, x in enumerate(span):
            here = found[q * depth : (q + 1) * depth]
            near_ref[x] = here[:, :width]
            if total_ref is not None:
                total = jnp.where(lane == x % LANES, here[:, width : width + LANES], total)
        if total_ref is not None and (start + CHUNK) % LANES == 0:
            total_ref[:, start + CHUNK - LANES : start + CHUNK] = total


def out_copies(source_ref, out_hbm, sems, ends, chunk):
    start = ends[chunk - 1] if chunk else 0
    span = pl.ds(start, ends[chunk] - start)
    return [
        pltpu.make_async_copy(source_ref.at[:, span, z, :], out_hbm.at[:, z, span, :], sems.at[chunk])
        for z in range(out_hbm.shape[1])
    ]


def out_ends(rows):
    return [8, 16] + list(range(CHUNK, rows + 1, CHUNK))


def mix_body(
    scale_line, count, plane_ref, gain_ref, shift_ref, rest_ref, fluor_ref, near_ref,
    out_ref, last_ref, grad_hbm, sems,
):
    n_energy, rows, _, _ = rest_ref.shape
    n_species = out_ref.shape[0]
    sigma, line = planes(plane_ref, n_species, n_energy)
    mixed = [[sigma[s][e] * gain_ref[e] for e in range(n_energy)] for s in range(n_species)]
    shift = [shift_ref[s] for s in range(n_species)]
    place = lax.axis_index("det")

    @pl.when(place == 0)
    def _():
        ends = out_ends(rows)
        scaled = [v * scale_line for v in line]
        for x in range(rows):
            rest = [rest_ref[e, x] for e in range(n_energy)]
            before = near_ref[x]
            for s in range(n_species):
                out_ref[s, x] = weighted(mixed[s], rest) + (shift[s] + scaled[s] * before)
            if x + 1 in ends:
                for copy in out_copies(out_ref, grad_hbm, sems, ends, ends.index(x + 1)):
                    copy.start()
        for chunk in range(len(ends)):
            for copy in out_copies(out_ref, grad_hbm, sems, ends, chunk):
                copy.wait()

    @pl.when(place != 0)
    def _():
        def step(block, carry):
            for q in range(STEP):
                x = block * STEP + q
                rest = [rest_ref[e, x] for e in range(n_energy)]
                for s in range(n_species):
                    out_ref[s, x] = weighted(mixed[s], rest) + shift[s]
            return carry

        lax.fori_loop(0, rows // STEP, step, 0)

    if count > 1:

        @pl.when(place == count - 1)
        def _():
            column_sums([gain_ref[e] for e in range(n_energy)], fluor_ref, last_ref, None)


def finish_body(
    scale, scale_line, count, plane_ref, nearer_ref, near_ref, last_ref, mix_ref, fan_ref, measured_ref, grad_in, *refs
):
    lines, (grad_hbm, residual_hbm, grad_ref, residual_ref, sems, residual_sem) = refs[:-6], refs[-6:]
    n_species, rows, depth, width = mix_ref.shape
    n_energy, share, _ = residual_ref.shape
    place = lax.axis_index("det")
    ends = out_ends(rows)

    @pl.when(place != 0)
    def _():
        line = [v * scale_line for v in planes(plane_ref, n_species, n_energy)[1]]
        last = place == count - 1
        for x, column in columns(nearer_ref, lambda v: v, width):
            before = jnp.where(last, last_ref[x], near_ref[x]) + column
            for s in range(n_species):
                grad_ref[s, x] = mix_ref[s, x] + line[s] * before
            if x + 1 in ends:
                for copy in out_copies(grad_ref, grad_hbm, sems, ends, ends.index(x + 1)):
                    copy.start()

    start = pl.multiple_of(lax.axis_index(("beam", "slab")) * share, share)
    pieces = [(ref, i) for ref in lines for i in range(ref.shape[0])]
    pieces = [(r, ref, i) for r, (ref, i) in enumerate(pieces)]
    sums = weigh(fan_ref[pl.ds(start, share), :], pieces, depth, n_energy, width)
    for e in range(n_energy):
        residual_ref[e] = sums[e] * scale - measured_ref[e, pl.ds(start, share), :]
    copy = pltpu.make_async_copy(residual_ref, residual_hbm, residual_sem)
    copy.start()

    @pl.when(place != 0)
    def _():
        for chunk in range(len(ends)):
            for done in out_copies(grad_ref, grad_hbm, sems, ends, chunk):
                done.wait()

    copy.wait()


def odd_pairs(n_beam, n_slab):
    pairs = []
    for beam in range(n_beam):
        for slab in range(n_slab):
            other = slab + 1 if slab % 2 else slab - 1
            if 0 <= other < n_slab:
                target = beam * n_slab + other
            else:
                target = (beam ^ 1) * n_slab + slab
            pairs.append((beam * n_slab + slab, target))
    return pairs


def swap(value, axis, distance):
    return lax.ppermute(value, axis, [(i, i ^ distance) for i in range(lax.axis_size(axis))])


def beyond(value, axis, backward):
    count = lax.axis_size(axis)
    if count == 2:
        return swap(value, axis, 1)
    mine = lax.axis_index(axis)
    pieces = lax.all_gather(value, axis)
    places = jnp.arange(count)
    keep = (places < mine) if backward else (places > mine)
    return jnp.sum(jnp.where(keep.reshape((-1,) + (1,) * value.ndim), pieces, 0.0), axis=0)


def shards(conc, cross, line, index, fan_offset, fan_weight, measured):
    n_species, depth, rows, width = conc.shape
    n_energy = index.shape[0]
    n_beam, n_det, n_slab = (lax.axis_size(a) for a in ("beam", "det", "slab"))
    assert n_beam & (n_beam - 1) == 0 and n_slab & (n_slab - 1) == 0
    assert fan_weight.shape[1] <= depth + 1
    assert rows % LANES == 0 and width % LANES == 0 and depth % 8 == 0
    full_x, full_y = rows * n_beam, width * n_det
    scale_x = -(1.5 / full_x) * LOG2E
    scale_y = -(1.5 / full_y) * LOG2E
    scale_sum = 1.0 / (scale_x * full_x)
    voxels = depth * rows * width
    turned = (n_species, rows, depth, width)
    cube = VMEM((n_energy, rows, depth, width), F32)
    plane = VMEM((rows, depth, width), F32)

    n_early = (n_energy + 3) // 4
    conc_x, emission, far_local, row_total, fixed = call(
        functools.partial(load_body, scale_y, scale_x),
        (VMEM(turned, F32), VMEM((n_early, rows, depth, width), F32), plane, plain(depth, rows),
         VMEM((n_species * n_energy + n_species, depth, width), F32)),
        (VMEM,) * 5,
        (HBM,) * 4,
        [
            SMEM(line.shape, F32),
            SMEM(cross.shape, F32),
            SMEM(index.shape, index.dtype),
            pltpu.SemaphoreType.DMA((3,)),
            pltpu.SemaphoreType.DMA((rows // CHUNK + 1,)),
        ],
        cost=(40 * voxels, 0, 16 * voxels),
    )(*(pltpu.with_memory_space_constraint(v, HBM) for v in (line, cross, index, conc)))

    far = beyond(row_total, "det", False)

    trans, emit, local_pair = call(
        functools.partial(local_body, scale_x),
        (cube, cube, plain(2, n_energy, depth, width)),
        (VMEM, VMEM, VMEM),
        (VMEM,) * 4,
        cost=(20 * voxels, 4 * voxels, 1024),
    )(fixed, conc_x, emission, far_local)

    wide = (n_energy, depth, width)
    far_wide, pair = call(
        functools.partial(line_body, n_det), (plane, plain(2, *wide)), (VMEM,) * 2, (VMEM,) * 3,
        cost=(8 * voxels, 0, 1024),
    )(far, emit, local_pair)

    fluor, rest = call(
        functools.partial(ahead_body, n_det), (cube, cube), (VMEM, VMEM), (VMEM, VMEM, VMEM),
        cost=(20 * voxels, 0, 1024),
    )(far_wide, trans, emit)

    others = []
    for r in range(1, n_beam):
        others.append(swap(pair, "beam", r))
    if others:
        others[-1], fluor, rest = lax.optimization_barrier((others[-1], fluor, rest))
    total, up, further = call(
        merge_body, (plain(1, *wide), plain(*wide), plain(*wide)), (VMEM,) * 3, (VMEM,) * n_beam,
        cost=(1 << 15, 1 << 13, 1024),
    )(pair, *others)

    if n_slab == 4 and n_beam > 1:
        even = swap(total, "slab", 1)
        odd = lax.ppermute(total, ("beam", "slab"), odd_pairs(n_beam, n_slab))
        near_lines = [total, even, odd]
        near_slabs = [0, 1, None]
        half = jnp.concatenate([total, even], axis=0)
        lines = [total, even, swap(half, "slab", 2)]
    else:
        lines = [total] + [swap(total, "slab", r) for r in range(1, n_slab)]
        near_slabs = [r for r in range(n_slab) if r & (r + 1) == 0]
        near_lines = [lines[r] for r in near_slabs]

    pixels = fan_offset.shape[0]
    gram, pull, fan_turned = call(
        functools.partial(fan_body, scale_sum, near_slabs), (plain(depth, depth * len(near_slabs)), plain(*wide), plain(pixels, depth * n_slab)),
        (VMEM,) * 3, (VMEM,) * 4, cost=(8 * depth * measured.size, 0, 4 * measured.size),
    )(fan_offset[None, :], fan_weight.T, measured, total)

    near, column_total, gain, shift = call(
        functools.partial(back_body, scale_sum, n_det),
        (plane, plain(depth, rows), plain(*wide), plain(n_species, depth, width)),
        (VMEM,) * 4,
        (VMEM,) * (5 + len(near_lines)),
        cost=(10 * voxels, 0, 1024),
    )(fixed, gram, pull, up, further, fluor, *near_lines[1:])

    nearer = beyond(column_total, "det", True)

    scale_line = scale_y * LN2 / scale_x
    out_sems = pltpu.SemaphoreType.DMA((len(out_ends(rows)),))
    mixed, near_last, grad = call(
        functools.partial(mix_body, scale_line, n_det),
        (VMEM(turned, F32), plane, HBM(conc.shape, F32)),
        (VMEM, VMEM, HBM),
        (VMEM,) * 6,
        [out_sems],
        cost=(40 * voxels, 0, 1024),
    )(fixed, gain, shift, rest, fluor, near)

    share = pixels // (n_beam * n_slab)
    return tuple(
        call(
            functools.partial(finish_body, scale_sum, scale_line, n_det),
            (plain(*conc.shape), plain(n_energy, share, width)),
            (HBM, HBM),
            (VMEM,) * 7 + (HBM,) + (VMEM,) * len(lines),
            [VMEM(turned, F32), VMEM((n_energy, share, width), F32), out_sems, pltpu.SemaphoreType.DMA],
            limit=16,
            cost=(10 * voxels, 0, 16 * voxels),
            aliases={7: 0},
        )(fixed, nearer, near, near_last, mixed, fan_turned, measured, grad, *lines)
    )


def solution(mesh):
    in_specs = (P(None, "slab", "beam", "det"), P(), P(), P(), P(), P(), P(None, None, "det"))
    out_specs = (P(None, "slab", "beam", "det"), P(None, ("beam", "slab"), "det"))
    return jax.shard_map(shards, mesh=mesh, in_specs=in_specs, out_specs=out_specs, check_vma=False)
```

profile of v0, /device:TPU:12, one launch (start us, length us, event | category | flops | bytes accessed | tf_op | source)
XLA Modules:
  0.0 29.2 jit_solution(8488469501534328608)
XLA Ops:
  0.6 3.1 %shard_map.86 = (f32[4,256,8,128]{3,2,1,0:T(8,128)S(1)}, f32[1,256,8,128]{3,2,1,0:T(8,128)S(1)}, f32[256,8,128]{2,1,0:T(8,128)S(1)}, f32[8,256]{1,0:T(8,128)S(1)}, f32[20,8,128]{2,1,0:T(8,128)S(1)}) custom-call(f32[4]{0:T(128)} %line_hbm.1, f32[4,16]{1,0:T(4,128)} %cross_hbm.1, s32[4]{0:T(128)} %index_hbm.1, f32[4,8,256,128]{3,2,1,0:T(8,128)} %conc_hbm.1), custom_call_target="tpu_custom_call" | custom-call | flops 10485760 | bytes 4194304 | tf_op jit(solution)/shard_map/pallas_call | solution.py:461
  3.7 0.6 %collective-permute-start = (f32[8,256]{1,0:T(8,128)S(1)}, f32[8,256]{1,0:T(8,128)S(1)}, u32[]{:S(2)}, u32[]{:S(2)}) collective-permute-start(f32[8,256]{1,0:T(8,128)S(1)} %get-tuple-element.31), channel_id=1, source_target_pairs={{0,4},{4,0},{1,5},{5,1},{2,6},{6,2},{3,7},{7,3},{8,12},{12,8},{9,1... | collective-permute-start | bytes 24584 | tf_op jit(solution)/shard_map/ppermute | solution.py:430
  4.3 1.5 %shard_map.87 = (f32[4,256,8,128]{3,2,1,0:T(8,128)S(1)}, f32[4,256,8,128]{3,2,1,0:T(8,128)S(1)}, f32[2,4,8,128]{3,2,1,0:T(8,128)S(1)}) custom-call(f32[20,8,128]{2,1,0:T(8,128)S(1)} %get-tuple-element.30.plane_ref, f32[4,256,8,128]{3,2,1,0:T(8,128)S(1)} %get-tuple-element.32.conc_ref, f32[1,256,8,128]{3,2,1,0:T(8,128)S(1)} %get-tuple-element.33.early_ref, ...), custom_call_target="tpu_custom_call" | custom-call | flops 5242880 | bytes 1024 | tf_op jit(solution)/shard_map/pallas_call | solution.py:479
  5.8 1.6 %collective-permute-done.far_ref = f32[8,256]{1,0:T(8,128)S(1)} collective-permute-done((f32[8,256]{1,0:T(8,128)S(1)}, f32[8,256]{1,0:T(8,128)S(1)}, u32[]{:S(2)}, u32[]{:S(2)}) %collective-permute-start) | collective-permute-done | bytes 8224 | tf_op jit(solution)/shard_map/ppermute | solution.py:430
  7.4 0.0 collective-permute-start.3
  7.4 1.6 %collective-permute-start.1 = (f32[2,4,8,128]{3,2,1,0:T(8,128)S(1)}, f32[2,4,8,128]{3,2,1,0:T(8,128)S(1)}, u32[]{:S(2)}, u32[]{:S(2)}) collective-permute-start(f32[2,4,8,128]{3,2,1,0:T(8,128)S(1)} %get-tuple-element.37.refs_0_), channel_id=1, source_target_pairs={{0,8},{8,0},{16,24},{24,16},{1,9},{9,1},{17,25},{25,17},{2,10},{10... | collective-permute-start | bytes 98312 | tf_op jit(solution)/shard_map/ppermute | solution.py:430
  9.0 0.5 %collective-permute-start.2 = (f32[2,4,8,128]{3,2,1,0:T(8,128)S(1)}, f32[2,4,8,128]{3,2,1,0:T(8,128)S(1)}, u32[]{:S(2)}, u32[]{:S(2)}) collective-permute-start(f32[2,4,8,128]{3,2,1,0:T(8,128)S(1)} %get-tuple-element.37.refs_0_), channel_id=1, source_target_pairs={{0,16},{8,24},{16,0},{24,8},{1,17},{9,25},{17,1},{25,9},{2,18},{10... | collective-permute-start | bytes 98312 | tf_op jit(solution)/shard_map/ppermute | solution.py:430
  9.6 0.0 copy-start
  9.6 0.0 copy-start.1
  9.6 0.0 copy-start.2
  9.6 1.7 %shard_map.89 = (f32[4,256,8,128]{3,2,1,0:T(8,128)S(1)}, f32[4,256,8,128]{3,2,1,0:T(8,128)S(1)}) custom-call(f32[256,8,128]{2,1,0:T(8,128)S(1)} %get-tuple-element.38.far_ref, f32[4,256,8,128]{3,2,1,0:T(8,128)S(1)} %get-tuple-element.39.trans_ref, f32[4,256,8,128]{3,2,1,0:T(8,128)S(1)} %get-tuple-element.35.emit_ref), custom_call_target="tpu_custom_call" | custom-call | flops 5242880 | bytes 1024 | tf_op jit(solution)/shard_map/pallas_call | solution.py:493
  11.2 0.0 collective-permute-done.3.refs_3_
  11.2 0.0 collective-permute-done.1.refs_1_
  11.3 1.7 %collective-permute-done.2.refs_2_ = f32[2,4,8,128]{3,2,1,0:T(8,128)S(1)} collective-permute-done((f32[2,4,8,128]{3,2,1,0:T(8,128)S(1)}, f32[2,4,8,128]{3,2,1,0:T(8,128)S(1)}, u32[]{:S(2)}, u32[]{:S(2)}) %collective-permute-start.2) | collective-permute-done | bytes 32800 | tf_op jit(solution)/shard_map/ppermute | solution.py:430
  13.0 0.5 %collective-permute-start.4 = (f32[1,4,8,128]{3,2,1,0:T(8,128)S(1)}, f32[1,4,8,128]{3,2,1,0:T(8,128)S(1)}, u32[]{:S(2)}, u32[]{:S(2)}) collective-permute-start(f32[1,4,8,128]{3,2,1,0:T(8,128)S(1)} %get-tuple-element.43.own_ref.refs_0_), channel_id=1, source_target_pairs={{0,1},{1,0},{2,3},{3,2},{4,5},{5,4},{6,7},{7,6},{8,9},{9,8},{10,11... | collective-permute-start | bytes 49160 | tf_op jit(solution)/shard_map/ppermute | solution.py:430
  13.5 3.3 %collective-permute-done.4.refs_0_.refs_1_ = f32[1,4,8,128]{3,2,1,0:T(8,128)S(1)} collective-permute-done((f32[1,4,8,128]{3,2,1,0:T(8,128)S(1)}, f32[1,4,8,128]{3,2,1,0:T(8,128)S(1)}, u32[]{:S(2)}, u32[]{:S(2)}) %collective-permute-start.4) | collective-permute-done | bytes 16416 | tf_op jit(solution)/shard_map/ppermute | solution.py:430
  16.8 2.6 %collective-permute-start.7 = (f32[2,4,8,128]{3,2,1,0:T(8,128)S(1)}, f32[2,4,8,128]{3,2,1,0:T(8,128)S(1)}, u32[]{:S(2)}, u32[]{:S(2)}) collective-permute-start(f32[2,4,8,128]{3,2,1,0:T(8,128)S(1)} %pad_maximum_fusion), channel_id=1, source_target_pairs={{0,2},{1,3},{2,0},{3,1},{4,6},{5,7},{6,4},{7,5},{8,10},{9,11},{10,... | collective-permute-start | bytes 98312 | tf_op jit(solution)/shard_map/ppermute | solution.py:430
  19.4 0.0 collective-permute-start.5
  19.4 0.0 copy-done
  19.4 0.0 copy-done.1
  19.4 0.0 copy-done.2
  19.4 0.4 %shard_map.91 = (f32[8,24]{1,0:T(8,128)S(1)}, f32[4,8,128]{2,1,0:T(8,128)S(1)}, f32[256,32]{1,0:T(8,128)S(1)}) custom-call(s32[1,256]{1,0:T(1,128)S(1)} %bitcast.3, s32[4,256]{1,0:T(4,128)S(1)} %bitcast.2, f32[4,256,128]{2,1,0:T(8,128)S(1)} %copy-done, f32[1,4,8,128]{3,2,1,0:T(8,128)S(1)} %get-tuple-element.43.own_ref.refs_0_), custom_call_target="tpu_custom_call" | custom-call | flops 8388608 | bytes 524288 | tf_op jit(solution)/shard_map/pallas_call | solution.py:521
  19.8 3.4 %collective-permute-done.5.refs_1_ = f32[1,4,8,128]{3,2,1,0:T(8,128)S(1)} collective-permute-done((f32[1,4,8,128]{3,2,1,0:T(8,128)S(1)}, f32[1,4,8,128]{3,2,1,0:T(8,128)S(1)}, u32[]{:S(2)}, u32[]{:S(2)}) %collective-permute-start.5) | collective-permute-done | bytes 16416 | tf_op jit(solution)/shard_map/ppermute | solution.py:510
  23.1 0.1 shard_map.92
  23.2 1.7 %collective-permute-start.6 = (f32[8,256]{1,0:T(8,128)S(1)}, f32[8,256]{1,0:T(8,128)S(1)}, u32[]{:S(2)}, u32[]{:S(2)}) collective-permute-start(f32[8,256]{1,0:T(8,128)S(1)} %get-tuple-element.49), channel_id=1, source_target_pairs={{0,4},{4,0},{1,5},{5,1},{2,6},{6,2},{3,7},{7,3},{8,12},{12,8},{9,1... | collective-permute-start | bytes 24584 | tf_op jit(solution)/shard_map/ppermute | solution.py:430
  24.9 1.8 %shard_map.93 = (f32[4,256,8,128]{3,2,1,0:T(8,128)S(1)}, f32[256,8,128]{2,1,0:T(8,128)S(1)}, f32[4,8,256,128]{3,2,1,0:T(8,128)}) custom-call(f32[20,8,128]{2,1,0:T(8,128)S(1)} %get-tuple-element.30.plane_ref, f32[4,8,128]{2,1,0:T(8,128)S(1)} %get-tuple-element.51.gain_ref, f32[4,8,128]{2,1,0:T(8,128)S(1)} %get-tuple-element.52.shift_ref, ...), custom_call_target="tpu_custom_call" | custom-call | flops 10485760 | bytes 1024 | tf_op jit(solution)/shard_map/pallas_call | solution.py:538
  26.7 0.2 collective-permute-done.6.nearer_ref
  26.9 0.0 collective-permute-done.7.refs_2_
  26.9 2.3 %shard_map.94 = (f32[4,8,256,128]{3,2,1,0:T(8,128)}, f32[4,16,128]{2,1,0:T(8,128)}) custom-call(f32[20,8,128]{2,1,0:T(8,128)S(1)} %get-tuple-element.30.plane_ref, f32[8,256]{1,0:T(8,128)S(1)} %collective-permute-done.6.nearer_ref, f32[256,8,128]{2,1,0:T(8,128)S(1)} %get-tuple-element.50.near_ref, ...), custom_call_target="tpu_custom_call", output_to_operand_aliasing={{0}: (7, {})} | custom-call | flops 2621440 | bytes 4194304 | tf_op jit(solution)/shard_map/pallas_call | solution.py:549
  (3 shorter events, 0.0 us)
Async XLA Ops:
  3.7 3.7 %collective-permute-start = (f32[8,256]{1,0:T(8,128)S(1)}, f32[8,256]{1,0:T(8,128)S(1)}, u32[]{:S(2)}, u32[]{:S(2)}) collective-permute-start(f32[8,256]{1,0:T(8,128)S(1)} %get-tuple-element.31), channel_id=1, source_target_pairs={{0,4},{4,0},{1,5},{5,1},{2,6},{6,2},{3,7},{7,3},{8,12},{12,8},{9,1... | collective-permute-start | bytes 24584 | tf_op jit(solution)/shard_map/ppermute | solution.py:430
  7.4 3.8 %collective-permute-start.3 = (f32[2,4,8,128]{3,2,1,0:T(8,128)S(1)}, f32[2,4,8,128]{3,2,1,0:T(8,128)S(1)}, u32[]{:S(2)}, u32[]{:S(2)}) collective-permute-start(f32[2,4,8,128]{3,2,1,0:T(8,128)S(1)} %get-tuple-element.37.refs_0_), channel_id=1, source_target_pairs={{0,24},{8,16},{16,8},{24,0},{1,25},{9,17},{17,9},{25,1},{2,26},{10... | collective-permute-start | bytes 98312 | tf_op jit(solution)/shard_map/ppermute | solution.py:430
  7.4 3.8 %collective-permute-start.1 = (f32[2,4,8,128]{3,2,1,0:T(8,128)S(1)}, f32[2,4,8,128]{3,2,1,0:T(8,128)S(1)}, u32[]{:S(2)}, u32[]{:S(2)}) collective-permute-start(f32[2,4,8,128]{3,2,1,0:T(8,128)S(1)} %get-tuple-element.37.refs_0_), channel_id=1, source_target_pairs={{0,8},{8,0},{16,24},{24,16},{1,9},{9,1},{17,25},{25,17},{2,10},{10... | collective-permute-start | bytes 98312 | tf_op jit(solution)/shard_map/ppermute | solution.py:430
  9.0 3.9 %collective-permute-start.2 = (f32[2,4,8,128]{3,2,1,0:T(8,128)S(1)}, f32[2,4,8,128]{3,2,1,0:T(8,128)S(1)}, u32[]{:S(2)}, u32[]{:S(2)}) collective-permute-start(f32[2,4,8,128]{3,2,1,0:T(8,128)S(1)} %get-tuple-element.37.refs_0_), channel_id=1, source_target_pairs={{0,16},{8,24},{16,0},{24,8},{1,17},{9,25},{17,1},{25,9},{2,18},{10... | collective-permute-start | bytes 98312 | tf_op jit(solution)/shard_map/ppermute | solution.py:430
  9.6 9.8 %copy-start = (f32[4,256,128]{2,1,0:T(8,128)S(1)}, f32[4,256,128]{2,1,0:T(8,128)}, u32[]{:S(2)}) copy-start(f32[4,256,128]{2,1,0:T(8,128)} %measured_ref.3) | copy-start | bytes 1572868
  9.6 9.8 %copy-start.1 = (s32[256,4]{0,1:T(4,128)S(1)}, s32[256,4]{0,1:T(4,128)}, u32[]{:S(2)}) copy-start(s32[256,4]{0,1:T(4,128)} %param.12) | copy-start | bytes 12292
  9.6 9.8 %copy-start.2 = (s32[256]{0:T(256)S(1)}, s32[256]{0:T(256)}, u32[]{:S(2)}) copy-start(s32[256]{0:T(256)} %param.11) | copy-start | bytes 3076
  13.0 3.8 %collective-permute-start.4 = (f32[1,4,8,128]{3,2,1,0:T(8,128)S(1)}, f32[1,4,8,128]{3,2,1,0:T(8,128)S(1)}, u32[]{:S(2)}, u32[]{:S(2)}) collective-permute-start(f32[1,4,8,128]{3,2,1,0:T(8,128)S(1)} %get-tuple-element.43.own_ref.refs_0_), channel_id=1, source_target_pairs={{0,1},{1,0},{2,3},{3,2},{4,5},{5,4},{6,7},{7,6},{8,9},{9,8},{10,11... | collective-permute-start | bytes 49160 | tf_op jit(solution)/shard_map/ppermute | solution.py:430
  16.8 10.2 %collective-permute-start.7 = (f32[2,4,8,128]{3,2,1,0:T(8,128)S(1)}, f32[2,4,8,128]{3,2,1,0:T(8,128)S(1)}, u32[]{:S(2)}, u32[]{:S(2)}) collective-permute-start(f32[2,4,8,128]{3,2,1,0:T(8,128)S(1)} %pad_maximum_fusion), channel_id=1, source_target_pairs={{0,2},{1,3},{2,0},{3,1},{4,6},{5,7},{6,4},{7,5},{8,10},{9,11},{10,... | collective-permute-start | bytes 98312 | tf_op jit(solution)/shard_map/ppermute | solution.py:430
  19.4 3.7 %collective-permute-start.5 = (f32[1,4,8,128]{3,2,1,0:T(8,128)S(1)}, f32[1,4,8,128]{3,2,1,0:T(8,128)S(1)}, u32[]{:S(2)}, u32[]{:S(2)}) collective-permute-start(f32[1,4,8,128]{3,2,1,0:T(8,128)S(1)} %get-tuple-element.43.own_ref.refs_0_), channel_id=1, source_target_pairs={{0,8},{1,2},{2,1},{3,11},{8,0},{9,10},{10,9},{11,3},{16,24},{17,18... | collective-permute-start | bytes 49160 | tf_op jit(solution)/shard_map/ppermute | solution.py:510
  23.2 3.7 %collective-permute-start.6 = (f32[8,256]{1,0:T(8,128)S(1)}, f32[8,256]{1,0:T(8,128)S(1)}, u32[]{:S(2)}, u32[]{:S(2)}) collective-permute-start(f32[8,256]{1,0:T(8,128)S(1)} %get-tuple-element.49), channel_id=1, source_target_pairs={{0,4},{4,0},{1,5},{5,1},{2,6},{6,2},{3,7},{7,3},{8,12},{12,8},{9,1... | collective-permute-start | bytes 24584 | tf_op jit(solution)/shard_map/ppermute | solution.py:430
where the time goes:
time: 29.4 us; the launch traced here: 29.2 us
  Pallas kernels  10.8 us (37%)
  waiting for transfers between devices  10.2 us (35%)
  starting transfers between devices  7.55 us (26%)
  between operations  0.71 us (2%)
    ppermute x7, starting transfers between devices, swap(): lax.ppermute(value, axis, [(i, i ^ distance) for i in range(lax.axis_size...  7.54 us
    ppermute x7, waiting for transfers between devices, swap(): lax.ppermute(value, axis, [(i, i ^ distance) for i in range(lax.axis_size...  6.8 us
    ppermute x1, waiting for transfers between devices, shards(): odd = lax.ppermute(total, ('beam', 'slab'), odd_pairs(n_beam, n_slab))  3.35 us
    pallas_call x1, Pallas kernels, shards(): call(functools.partial(load_body, scale_y, scale_x), (VMEM(turned, F32),...  3.06 us
    pallas_call x1, Pallas kernels, shards(): call(functools.partial(finish_body, scale_sum, scale_line, n_det), (plain...  2.28 us
    pallas_call x1, Pallas kernels, shards(): call(functools.partial(mix_body, scale_line, n_det), (VMEM(turned, F32),...  1.76 us
    pallas_call x1, Pallas kernels, shards(): call(functools.partial(ahead_body, n_det), (cube, cube), (VMEM, VMEM), (V...  1.66 us
    pallas_call x1, Pallas kernels, shards(): call(functools.partial(local_body, scale_x), (cube, cube, plain(2, n_ener...  1.53 us
  transfers between devices with their start and end apart: 8, of which 5 were waited for; matrix products, arithmetic and copies ran while one was open for 0% of the time, Pallas kernels for 19%

commit v1 on v0

--- a/solution.py
+++ b/solution.py
@@ -68,21 +68,19 @@
     return total
 
 
+def in_ends(rows):
+    return [rows * part // 16 for part in (6, 10, 13, 15, 16)]
+
+
 def load_body(
     scale, scale_x, line_hbm, cross_hbm, index_hbm, conc_hbm, conc_ref, emit_ref, beyond_ref, total_ref, plane_ref,
     line_ref, cross_ref, index_ref, small_sems, sems,
 ):
     n_species, depth, rows, width = conc_hbm.shape
     n_early = emit_ref.shape[0]
-    ends = list(range(CHUNK, rows, CHUNK)) + [rows - CHUNK // 2, rows]
+    ends = in_ends(rows)
     starts = [0] + ends[:-1]
-
-    def copies(chunk):
-        span = pl.ds(starts[chunk], ends[chunk] - starts[chunk])
-        return [
-            pltpu.make_async_copy(conc_hbm.at[:, z, span, :], conc_ref.at[:, span, z, :], sems.at[chunk])
-            for z in range(depth)
-        ]
+    spans = [pl.ds(start, end - start) for start, end in zip(starts, ends)]
 
     small = [
         pltpu.make_async_copy(source, target, small_sems.at[i])
@@ -92,9 +90,11 @@
     ]
     for copy in small:
         copy.start()
-    for chunk in range(len(ends)):
-        for copy in copies(chunk):
-            copy.start()
+    for chunk, span in enumerate(spans):
+        for z in range(depth):
+            pltpu.make_async_copy(
+                conc_hbm.at[:, z, span, :], conc_ref.at[:, span, z, :], sems.at[chunk]
+            ).start()
     table = lane_sums(width, True)
     lane = lax.broadcasted_iota(jnp.int32, (depth, LANES), 1)
     for copy in small:
@@ -107,8 +107,8 @@
     sigma = [[v * scale_x for v in row] for row in sigma]
     total = jnp.zeros((depth, LANES), F32)
     for chunk, (start, end) in enumerate(zip(starts, ends)):
-        for copy in copies(chunk):
-            copy.wait()
+        whole = conc_ref.at[:, spans[chunk]]
+        pltpu.make_async_copy(whole, whole, sems.at[chunk]).wait()
         absorber = []
         for x in range(start, end):
             conc = [conc_ref[s, x] for s in range(n_species)]
@@ -120,8 +120,8 @@
             here = sums[q * depth : (q + 1) * depth]
             beyond_ref[x] = here[:, :width]
             total = jnp.where(lane == x % LANES, here[:, width : width + LANES], total)
-        if end % LANES == 0:
-            total_ref[:, end - LANES : end] = total
+            if (x + 1) % LANES == 0:
+                total_ref[:, x + 1 - LANES : x + 1] = total
 
 
 def local_body(scale, plane_ref, conc_ref, early_ref, beyond_ref, trans_ref, emit_ref, pair_ref):
@@ -324,8 +324,14 @@
     ]
 
 
+def out_wait(source_ref, sems, ends, chunk):
+    start = ends[chunk - 1] if chunk else 0
+    whole = source_ref.at[:, pl.ds(start, ends[chunk] - start)]
+    pltpu.make_async_copy(whole, whole, sems.at[chunk]).wait()
+
+
 def out_ends(rows):
-    return [8, 16] + list(range(CHUNK, rows + 1, CHUNK))
+    return [rows * part // 16 for part in (1, 4, 8, 12, 16)]
 
 
 def mix_body(
@@ -352,8 +358,7 @@
                 for copy in out_copies(out_ref, grad_hbm, sems, ends, ends.index(x + 1)):
                     copy.start()
         for chunk in range(len(ends)):
-            for copy in out_copies(out_ref, grad_hbm, sems, ends, chunk):
-                copy.wait()
+            out_wait(out_ref, sems, ends, chunk)
 
     @pl.when(place != 0)
     def _():
@@ -407,8 +412,7 @@
     @pl.when(place != 0)
     def _():
         for chunk in range(len(ends)):
-            for done in out_copies(grad_ref, grad_hbm, sems, ends, chunk):
-                done.wait()
+            out_wait(grad_ref, sems, ends, chunk)
 
     copy.wait()
 
@@ -469,7 +473,7 @@
             SMEM(cross.shape, F32),
             SMEM(index.shape, index.dtype),
             pltpu.SemaphoreType.DMA((3,)),
-            pltpu.SemaphoreType.DMA((rows // CHUNK + 1,)),
+            pltpu.SemaphoreType.DMA((len(in_ends(rows)),)),
         ],
         cost=(40 * voxels, 0, 16 * voxels),
     )(*(pltpu.with_memory_space_constraint(v, HBM) for v in (line, cross, index, conc)))

time: 29.4 us -> 29.1 us (0.990)
  Pallas kernels: 10.8 us -> 10.5 us
where the time goes in v1:
time: 29.1 us; the launch traced here: 29 us
  Pallas kernels  10.5 us (36%)
  waiting for transfers between devices  10.2 us (35%)
  starting transfers between devices  7.55 us (26%)
  between operations  0.71 us (2%)
    ppermute x7, starting transfers between devices, swap(): lax.ppermute(value, axis, [(i, i ^ distance) for i in range(lax.axis_size...  7.54 us
    ppermute x7, waiting for transfers between devices, swap(): lax.ppermute(value, axis, [(i, i ^ distance) for i in range(lax.axis_size...  6.85 us
    ppermute x1, waiting for transfers between devices, shards(): odd = lax.ppermute(total, ('beam', 'slab'), odd_pairs(n_beam, n_slab))  3.35 us
    pallas_call x1, Pallas kernels, shards(): call(functools.partial(load_body, scale_y, scale_x), (VMEM(turned, F32),...  2.83 us
    pallas_call x1, Pallas kernels, shards(): call(functools.partial(finish_body, scale_sum, scale_line, n_det), (plain...  2.26 us
    pallas_call x1, Pallas kernels, shards(): call(functools.partial(mix_body, scale_line, n_det), (VMEM(turned, F32),...  1.72 us
    pallas_call x1, Pallas kernels, shards(): call(functools.partial(ahead_body, n_det), (cube, cube), (VMEM, VMEM), (V...  1.66 us
    pallas_call x1, Pallas kernels, shards(): call(functools.partial(local_body, scale_x), (cube, cube, plain(2, n_ener...  1.53 us
  transfers between devices with their start and end apart: 8, of which 5 were waited for; matrix products, arithmetic and copies ran while one was open for 0% of the time, Pallas kernels for 19%

profile of v1, /device:TPU:12, one launch (start us, length us, event | category | flops | bytes accessed | tf_op | source)
XLA Modules:
  0.0 29.0 jit_solution(824985594205678449)
XLA Ops:
  0.6 2.8 %shard_map.86 = (f32[4,256,8,128]{3,2,1,0:T(8,128)S(1)}, f32[1,256,8,128]{3,2,1,0:T(8,128)S(1)}, f32[256,8,128]{2,1,0:T(8,128)S(1)}, f32[8,256]{1,0:T(8,128)S(1)}, f32[20,8,128]{2,1,0:T(8,128)S(1)}) custom-call(f32[4]{0:T(128)} %line_hbm.1, f32[4,16]{1,0:T(4,128)} %cross_hbm.1, s32[4]{0:T(128)} %index_hbm.1, f32[4,8,256,128]{3,2,1,0:T(8,128)} %conc_hbm.1), custom_call_target="tpu_custom_call" | custom-call | flops 10485760 | bytes 4194304 | tf_op jit(solution)/shard_map/pallas_call | solution.py:465
  3.5 0.6 %collective-permute-start = (f32[8,256]{1,0:T(8,128)S(1)}, f32[8,256]{1,0:T(8,128)S(1)}, u32[]{:S(2)}, u32[]{:S(2)}) collective-permute-start(f32[8,256]{1,0:T(8,128)S(1)} %get-tuple-element.31), channel_id=1, source_target_pairs={{0,4},{4,0},{1,5},{5,1},{2,6},{6,2},{3,7},{7,3},{8,12},{12,8},{9,1... | collective-permute-start | bytes 24584 | tf_op jit(solution)/shard_map/ppermute | solution.py:434
  4.0 1.5 %shard_map.87 = (f32[4,256,8,128]{3,2,1,0:T(8,128)S(1)}, f32[4,256,8,128]{3,2,1,0:T(8,128)S(1)}, f32[2,4,8,128]{3,2,1,0:T(8,128)S(1)}) custom-call(f32[20,8,128]{2,1,0:T(8,128)S(1)} %get-tuple-element.30.plane_ref, f32[4,256,8,128]{3,2,1,0:T(8,128)S(1)} %get-tuple-element.32.conc_ref, f32[1,256,8,128]{3,2,1,0:T(8,128)S(1)} %get-tuple-element.33.early_ref, ...), custom_call_target="tpu_custom_call" | custom-call | flops 5242880 | bytes 1024 | tf_op jit(solution)/shard_map/pallas_call | solution.py:483
  5.6 1.6 %collective-permute-done.far_ref = f32[8,256]{1,0:T(8,128)S(1)} collective-permute-done((f32[8,256]{1,0:T(8,128)S(1)}, f32[8,256]{1,0:T(8,128)S(1)}, u32[]{:S(2)}, u32[]{:S(2)}) %collective-permute-start) | collective-permute-done | bytes 8224 | tf_op jit(solution)/shard_map/ppermute | solution.py:434
  7.2 0.0 collective-permute-start.3
  7.2 1.6 %collective-permute-start.1 = (f32[2,4,8,128]{3,2,1,0:T(8,128)S(1)}, f32[2,4,8,128]{3,2,1,0:T(8,128)S(1)}, u32[]{:S(2)}, u32[]{:S(2)}) collective-permute-start(f32[2,4,8,128]{3,2,1,0:T(8,128)S(1)} %get-tuple-element.37.refs_0_), channel_id=1, source_target_pairs={{0,8},{8,0},{16,24},{24,16},{1,9},{9,1},{17,25},{25,17},{2,10},{10... | collective-permute-start | bytes 98312 | tf_op jit(solution)/shard_map/ppermute | solution.py:434
  8.8 0.5 %collective-permute-start.2 = (f32[2,4,8,128]{3,2,1,0:T(8,128)S(1)}, f32[2,4,8,128]{3,2,1,0:T(8,128)S(1)}, u32[]{:S(2)}, u32[]{:S(2)}) collective-permute-start(f32[2,4,8,128]{3,2,1,0:T(8,128)S(1)} %get-tuple-element.37.refs_0_), channel_id=1, source_target_pairs={{0,16},{8,24},{16,0},{24,8},{1,17},{9,25},{17,1},{25,9},{2,18},{10... | collective-permute-start | bytes 98312 | tf_op jit(solution)/shard_map/ppermute | solution.py:434
  9.3 0.0 copy-start
  9.3 0.0 copy-start.1
  9.3 0.0 copy-start.2
  9.3 1.7 %shard_map.89 = (f32[4,256,8,128]{3,2,1,0:T(8,128)S(1)}, f32[4,256,8,128]{3,2,1,0:T(8,128)S(1)}) custom-call(f32[256,8,128]{2,1,0:T(8,128)S(1)} %get-tuple-element.38.far_ref, f32[4,256,8,128]{3,2,1,0:T(8,128)S(1)} %get-tuple-element.39.trans_ref, f32[4,256,8,128]{3,2,1,0:T(8,128)S(1)} %get-tuple-element.35.emit_ref), custom_call_target="tpu_custom_call" | custom-call | flops 5242880 | bytes 1024 | tf_op jit(solution)/shard_map/pallas_call | solution.py:497
  11.0 0.0 collective-permute-done.3.refs_3_
  11.0 0.0 collective-permute-done.1.refs_1_
  11.0 1.7 %collective-permute-done.2.refs_2_ = f32[2,4,8,128]{3,2,1,0:T(8,128)S(1)} collective-permute-done((f32[2,4,8,128]{3,2,1,0:T(8,128)S(1)}, f32[2,4,8,128]{3,2,1,0:T(8,128)S(1)}, u32[]{:S(2)}, u32[]{:S(2)}) %collective-permute-start.2) | collective-permute-done | bytes 32800 | tf_op jit(solution)/shard_map/ppermute | solution.py:434
  12.7 0.5 %collective-permute-start.4 = (f32[1,4,8,128]{3,2,1,0:T(8,128)S(1)}, f32[1,4,8,128]{3,2,1,0:T(8,128)S(1)}, u32[]{:S(2)}, u32[]{:S(2)}) collective-permute-start(f32[1,4,8,128]{3,2,1,0:T(8,128)S(1)} %get-tuple-element.43.own_ref.refs_0_), channel_id=1, source_target_pairs={{0,1},{1,0},{2,3},{3,2},{4,5},{5,4},{6,7},{7,6},{8,9},{9,8},{10,11... | collective-permute-start | bytes 49160 | tf_op jit(solution)/shard_map/ppermute | solution.py:434
  13.3 3.3 %collective-permute-done.4.refs_0_.refs_1_ = f32[1,4,8,128]{3,2,1,0:T(8,128)S(1)} collective-permute-done((f32[1,4,8,128]{3,2,1,0:T(8,128)S(1)}, f32[1,4,8,128]{3,2,1,0:T(8,128)S(1)}, u32[]{:S(2)}, u32[]{:S(2)}) %collective-permute-start.4) | collective-permute-done | bytes 16416 | tf_op jit(solution)/shard_map/ppermute | solution.py:434
  16.6 2.6 %collective-permute-start.7 = (f32[2,4,8,128]{3,2,1,0:T(8,128)S(1)}, f32[2,4,8,128]{3,2,1,0:T(8,128)S(1)}, u32[]{:S(2)}, u32[]{:S(2)}) collective-permute-start(f32[2,4,8,128]{3,2,1,0:T(8,128)S(1)} %pad_maximum_fusion), channel_id=1, source_target_pairs={{0,2},{1,3},{2,0},{3,1},{4,6},{5,7},{6,4},{7,5},{8,10},{9,11},{10,... | collective-permute-start | bytes 98312 | tf_op jit(solution)/shard_map/ppermute | solution.py:434
  19.1 0.0 collective-permute-start.5
  19.1 0.0 copy-done
  19.1 0.0 copy-done.1
  19.2 0.0 copy-done.2
  19.2 0.4 %shard_map.91 = (f32[8,24]{1,0:T(8,128)S(1)}, f32[4,8,128]{2,1,0:T(8,128)S(1)}, f32[256,32]{1,0:T(8,128)S(1)}) custom-call(s32[1,256]{1,0:T(1,128)S(1)} %bitcast.3, s32[4,256]{1,0:T(4,128)S(1)} %bitcast.2, f32[4,256,128]{2,1,0:T(8,128)S(1)} %copy-done, f32[1,4,8,128]{3,2,1,0:T(8,128)S(1)} %get-tuple-element.43.own_ref.refs_0_), custom_call_target="tpu_custom_call" | custom-call | flops 8388608 | bytes 524288 | tf_op jit(solution)/shard_map/pallas_call | solution.py:525
  19.5 3.4 %collective-permute-done.5.refs_1_ = f32[1,4,8,128]{3,2,1,0:T(8,128)S(1)} collective-permute-done((f32[1,4,8,128]{3,2,1,0:T(8,128)S(1)}, f32[1,4,8,128]{3,2,1,0:T(8,128)S(1)}, u32[]{:S(2)}, u32[]{:S(2)}) %collective-permute-start.5) | collective-permute-done | bytes 16416 | tf_op jit(solution)/shard_map/ppermute | solution.py:514
  22.9 0.1 shard_map.92
  23.0 1.7 %collective-permute-start.6 = (f32[8,256]{1,0:T(8,128)S(1)}, f32[8,256]{1,0:T(8,128)S(1)}, u32[]{:S(2)}, u32[]{:S(2)}) collective-permute-start(f32[8,256]{1,0:T(8,128)S(1)} %get-tuple-element.49), channel_id=1, source_target_pairs={{0,4},{4,0},{1,5},{5,1},{2,6},{6,2},{3,7},{7,3},{8,12},{12,8},{9,1... | collective-permute-start | bytes 24584 | tf_op jit(solution)/shard_map/ppermute | solution.py:434
  24.7 1.7 %shard_map.93 = (f32[4,256,8,128]{3,2,1,0:T(8,128)S(1)}, f32[256,8,128]{2,1,0:T(8,128)S(1)}, f32[4,8,256,128]{3,2,1,0:T(8,128)}) custom-call(f32[20,8,128]{2,1,0:T(8,128)S(1)} %get-tuple-element.30.plane_ref, f32[4,8,128]{2,1,0:T(8,128)S(1)} %get-tuple-element.51.gain_ref, f32[4,8,128]{2,1,0:T(8,128)S(1)} %get-tuple-element.52.shift_ref, ...), custom_call_target="tpu_custom_call" | custom-call | flops 10485760 | bytes 1024 | tf_op jit(solution)/shard_map/pallas_call | solution.py:542
  26.4 0.3 collective-permute-done.6.nearer_ref
  26.7 0.0 collective-permute-done.7.refs_2_
  26.7 2.3 %shard_map.94 = (f32[4,8,256,128]{3,2,1,0:T(8,128)}, f32[4,16,128]{2,1,0:T(8,128)}) custom-call(f32[20,8,128]{2,1,0:T(8,128)S(1)} %get-tuple-element.30.plane_ref, f32[8,256]{1,0:T(8,128)S(1)} %collective-permute-done.6.nearer_ref, f32[256,8,128]{2,1,0:T(8,128)S(1)} %get-tuple-element.50.near_ref, ...), custom_call_target="tpu_custom_call", output_to_operand_aliasing={{0}: (7, {})} | custom-call | flops 2621440 | bytes 4194304 | tf_op jit(solution)/shard_map/pallas_call | solution.py:553
  (3 shorter events, 0.0 us)
Async XLA Ops:
  3.5 3.7 %collective-permute-start = (f32[8,256]{1,0:T(8,128)S(1)}, f32[8,256]{1,0:T(8,128)S(1)}, u32[]{:S(2)}, u32[]{:S(2)}) collective-permute-start(f32[8,256]{1,0:T(8,128)S(1)} %get-tuple-element.31), channel_id=1, source_target_pairs={{0,4},{4,0},{1,5},{5,1},{2,6},{6,2},{3,7},{7,3},{8,12},{12,8},{9,1... | collective-permute-start | bytes 24584 | tf_op jit(solution)/shard_map/ppermute | solution.py:434
  7.2 3.8 %collective-permute-start.3 = (f32[2,4,8,128]{3,2,1,0:T(8,128)S(1)}, f32[2,4,8,128]{3,2,1,0:T(8,128)S(1)}, u32[]{:S(2)}, u32[]{:S(2)}) collective-permute-start(f32[2,4,8,128]{3,2,1,0:T(8,128)S(1)} %get-tuple-element.37.refs_0_), channel_id=1, source_target_pairs={{0,24},{8,16},{16,8},{24,0},{1,25},{9,17},{17,9},{25,1},{2,26},{10... | collective-permute-start | bytes 98312 | tf_op jit(solution)/shard_map/ppermute | solution.py:434
  7.2 3.8 %collective-permute-start.1 = (f32[2,4,8,128]{3,2,1,0:T(8,128)S(1)}, f32[2,4,8,128]{3,2,1,0:T(8,128)S(1)}, u32[]{:S(2)}, u32[]{:S(2)}) collective-permute-start(f32[2,4,8,128]{3,2,1,0:T(8,128)S(1)} %get-tuple-element.37.refs_0_), channel_id=1, source_target_pairs={{0,8},{8,0},{16,24},{24,16},{1,9},{9,1},{17,25},{25,17},{2,10},{10... | collective-permute-start | bytes 98312 | tf_op jit(solution)/shard_map/ppermute | solution.py:434
  8.8 3.9 %collective-permute-start.2 = (f32[2,4,8,128]{3,2,1,0:T(8,128)S(1)}, f32[2,4,8,128]{3,2,1,0:T(8,128)S(1)}, u32[]{:S(2)}, u32[]{:S(2)}) collective-permute-start(f32[2,4,8,128]{3,2,1,0:T(8,128)S(1)} %get-tuple-element.37.refs_0_), channel_id=1, source_target_pairs={{0,16},{8,24},{16,0},{24,8},{1,17},{9,25},{17,1},{25,9},{2,18},{10... | collective-permute-start | bytes 98312 | tf_op jit(solution)/shard_map/ppermute | solution.py:434
  9.3 9.8 %copy-start = (f32[4,256,128]{2,1,0:T(8,128)S(1)}, f32[4,256,128]{2,1,0:T(8,128)}, u32[]{:S(2)}) copy-start(f32[4,256,128]{2,1,0:T(8,128)} %measured_ref.3) | copy-start | bytes 1572868
  9.3 9.8 %copy-start.1 = (s32[256,4]{0,1:T(4,128)S(1)}, s32[256,4]{0,1:T(4,128)}, u32[]{:S(2)}) copy-start(s32[256,4]{0,1:T(4,128)} %param.12) | copy-start | bytes 12292
  9.3 9.8 %copy-start.2 = (s32[256]{0:T(256)S(1)}, s32[256]{0:T(256)}, u32[]{:S(2)}) copy-start(s32[256]{0:T(256)} %param.11) | copy-start | bytes 3076
  12.7 3.8 %collective-permute-start.4 = (f32[1,4,8,128]{3,2,1,0:T(8,128)S(1)}, f32[1,4,8,128]{3,2,1,0:T(8,128)S(1)}, u32[]{:S(2)}, u32[]{:S(2)}) collective-permute-start(f32[1,4,8,128]{3,2,1,0:T(8,128)S(1)} %get-tuple-element.43.own_ref.refs_0_), channel_id=1, source_target_pairs={{0,1},{1,0},{2,3},{3,2},{4,5},{5,4},{6,7},{7,6},{8,9},{9,8},{10,11... | collective-permute-start | bytes 49160 | tf_op jit(solution)/shard_map/ppermute | solution.py:434
  16.6 10.2 %collective-permute-start.7 = (f32[2,4,8,128]{3,2,1,0:T(8,128)S(1)}, f32[2,4,8,128]{3,2,1,0:T(8,128)S(1)}, u32[]{:S(2)}, u32[]{:S(2)}) collective-permute-start(f32[2,4,8,128]{3,2,1,0:T(8,128)S(1)} %pad_maximum_fusion), channel_id=1, source_target_pairs={{0,2},{1,3},{2,0},{3,1},{4,6},{5,7},{6,4},{7,5},{8,10},{9,11},{10,... | collective-permute-start | bytes 98312 | tf_op jit(solution)/shard_map/ppermute | solution.py:434
  19.1 3.7 %collective-permute-start.5 = (f32[1,4,8,128]{3,2,1,0:T(8,128)S(1)}, f32[1,4,8,128]{3,2,1,0:T(8,128)S(1)}, u32[]{:S(2)}, u32[]{:S(2)}) collective-permute-start(f32[1,4,8,128]{3,2,1,0:T(8,128)S(1)} %get-tuple-element.43.own_ref.refs_0_), channel_id=1, source_target_pairs={{0,8},{1,2},{2,1},{3,11},{8,0},{9,10},{10,9},{11,3},{16,24},{17,18... | collective-permute-start | bytes 49160 | tf_op jit(solution)/shard_map/ppermute | solution.py:514
  23.0 3.7 %collective-permute-start.6 = (f32[8,256]{1,0:T(8,128)S(1)}, f32[8,256]{1,0:T(8,128)S(1)}, u32[]{:S(2)}, u32[]{:S(2)}) collective-permute-start(f32[8,256]{1,0:T(8,128)S(1)} %get-tuple-element.49), channel_id=1, source_target_pairs={{0,4},{4,0},{1,5},{5,1},{2,6},{6,2},{3,7},{7,3},{8,12},{12,8},{9,1... | collective-permute-start | bytes 24584 | tf_op jit(solution)/shard_map/ppermute | solution.py:434

commit v2 on v1

--- a/solution.py
+++ b/solution.py
@@ -69,7 +69,7 @@
 
 
 def in_ends(rows):
-    return [rows * part // 16 for part in (6, 10, 13, 15, 16)]
+    return [rows * part // 16 for part in (4, 8, 12, 16)]
 
 
 def load_body(
@@ -379,12 +379,35 @@
             column_sums([gain_ref[e] for e in range(n_energy)], fluor_ref, last_ref, None)
 
 
+def residual_copy(scale, fan_ref, measured_ref, lines, residual_ref, residual_hbm, sem):
+    n_energy, share, width = residual_ref.shape
+    start = pl.multiple_of(lax.axis_index(("beam", "slab")) * share, share)
+    pieces = [(ref, i) for ref in lines for i in range(ref.shape[0])]
+    pieces = [(r, ref, i) for r, (ref, i) in enumerate(pieces)]
+    depth = fan_ref.shape[1] // len(pieces)
+    sums = weigh(fan_ref[pl.ds(start, share), :], pieces, depth, n_energy, width)
+    for e in range(n_energy):
+        residual_ref[e] = sums[e] * scale - measured_ref[e, pl.ds(start, share), :]
+    copy = pltpu.make_async_copy(residual_ref, residual_hbm, sem)
+    copy.start()
+    return copy
+
+
+def signal_body(scale, fan_ref, measured_ref, *refs):
+    lines, (residual_hbm, residual_ref, sem) = refs[:-3], refs[-3:]
+
+    @pl.when(lax.axis_index("det") == 0)
+    def _():
+        residual_copy(scale, fan_ref, measured_ref, lines, residual_ref, residual_hbm, sem).wait()
+
+
 def finish_body(
-    scale, scale_line, count, plane_ref, nearer_ref, near_ref, last_ref, mix_ref, fan_ref, measured_ref, grad_in, *refs
+    scale, scale_line, count, plane_ref, nearer_ref, near_ref, last_ref, mix_ref, fan_ref, measured_ref,
+    grad_in, residual_in, *refs,
 ):
     lines, (grad_hbm, residual_hbm, grad_ref, residual_ref, sems, residual_sem) = refs[:-6], refs[-6:]
-    n_species, rows, depth, width = mix_ref.shape
-    n_energy, share, _ = residual_ref.shape
+    n_species, rows, _, width = mix_ref.shape
+    n_energy = residual_ref.shape[0]
     place = lax.axis_index("det")
     ends = out_ends(rows)
 
@@ -399,22 +422,10 @@
             if x + 1 in ends:
                 for copy in out_copies(grad_ref, grad_hbm, sems, ends, ends.index(x + 1)):
                     copy.start()
-
-    start = pl.multiple_of(lax.axis_index(("beam", "slab")) * share, share)
-    pieces = [(ref, i) for ref in lines for i in range(ref.shape[0])]
-    pieces = [(r, ref, i) for r, (ref, i) in enumerate(pieces)]
-    sums = weigh(fan_ref[pl.ds(start, share), :], pieces, depth, n_energy, width)
-    for e in range(n_energy):
-        residual_ref[e] = sums[e] * scale - measured_ref[e, pl.ds(start, share), :]
-    copy = pltpu.make_async_copy(residual_ref, residual_hbm, residual_sem)
-    copy.start()
-
-    @pl.when(place != 0)
-    def _():
+        copy = residual_copy(scale, fan_ref, measured_ref, lines, residual_ref, residual_hbm, residual_sem)
         for chunk in range(len(ends)):
             out_wait(grad_ref, sems, ends, chunk)
-
-    copy.wait()
+        copy.wait()
 
 
 def odd_pairs(n_beam, n_slab):
@@ -549,17 +560,27 @@
     )(fixed, gain, shift, rest, fluor, near)
 
     share = pixels // (n_beam * n_slab)
+    residual_scratch = [VMEM((n_energy, share, width), F32), pltpu.SemaphoreType.DMA]
+    residual = call(
+        functools.partial(signal_body, scale_sum),
+        (HBM((n_energy, share, width), F32),),
+        (HBM,),
+        (VMEM,) * (2 + len(lines)),
+        residual_scratch,
+        cost=(1 << 16, 0, 1024),
+    )(fan_turned, measured, *lines)[0]
+
     return tuple(
         call(
             functools.partial(finish_body, scale_sum, scale_line, n_det),
             (plain(*conc.shape), plain(n_energy, share, width)),
             (HBM, HBM),
-            (VMEM,) * 7 + (HBM,) + (VMEM,) * len(lines),
-            [VMEM(turned, F32), VMEM((n_energy, share, width), F32), out_sems, pltpu.SemaphoreType.DMA],
+            (VMEM,) * 7 + (HBM,) * 2 + (VMEM,) * len(lines),
+            [VMEM(turned, F32), residual_scratch[0], out_sems, residual_scratch[1]],
             limit=16,
             cost=(10 * voxels, 0, 16 * voxels),
-            aliases={7: 0},
-        )(fixed, nearer, near, near_last, mixed, fan_turned, measured, grad, *lines)
+            aliases={7: 0, 8: 1},
+        )(fixed, nearer, near, near_last, mixed, fan_turned, measured, grad, residual, *lines)
     )
 
 

time: 29.1 us -> 28.8 us (0.990)
  Pallas kernels: 10.5 us -> 10.2 us
where the time goes in v2:
time: 28.8 us; the launch traced here: 28.7 us
  Pallas kernels  10.2 us (35%)
  waiting for transfers between devices  10.2 us (35%)
  starting transfers between devices  7.54 us (26%)
  between operations  0.73 us (3%)
    ppermute x7, starting transfers between devices, swap(): lax.ppermute(value, axis, [(i, i ^ distance) for i in range(lax.axis_size...  7.54 us
    ppermute x7, waiting for transfers between devices, swap(): lax.ppermute(value, axis, [(i, i ^ distance) for i in range(lax.axis_size...  6.8 us
    ppermute x1, waiting for transfers between devices, shards(): odd = lax.ppermute(total, ('beam', 'slab'), odd_pairs(n_beam, n_slab))  3.35 us
    pallas_call x1, Pallas kernels, shards(): call(functools.partial(load_body, scale_y, scale_x), (VMEM(turned, F32),...  2.62 us
    pallas_call x1, Pallas kernels, shards(): call(functools.partial(finish_body, scale_sum, scale_line, n_det), (plain...  2.16 us
    pallas_call x1, Pallas kernels, shards(): call(functools.partial(mix_body, scale_line, n_det), (VMEM(turned, F32),...  1.72 us
    pallas_call x1, Pallas kernels, shards(): call(functools.partial(ahead_body, n_det), (cube, cube), (VMEM, VMEM), (V...  1.66 us
    pallas_call x1, Pallas kernels, shards(): call(functools.partial(local_body, scale_x), (cube, cube, plain(2, n_ener...  1.53 us
  transfers between devices with their start and end apart: 8, of which 5 were waited for; matrix products, arithmetic and copies ran while one was open for 0% of the time, Pallas kernels for 19%

profile of v2, /device:TPU:12, one launch (start us, length us, event | category | flops | bytes accessed | tf_op | source)
XLA Modules:
  0.0 28.7 jit_solution(3800489401352012173)
XLA Ops:
  0.6 2.6 %shard_map.86 = (f32[4,256,8,128]{3,2,1,0:T(8,128)S(1)}, f32[1,256,8,128]{3,2,1,0:T(8,128)S(1)}, f32[256,8,128]{2,1,0:T(8,128)S(1)}, f32[8,256]{1,0:T(8,128)S(1)}, f32[20,8,128]{2,1,0:T(8,128)S(1)}) custom-call(f32[4]{0:T(128)} %line_hbm.1, f32[4,16]{1,0:T(4,128)} %cross_hbm.1, s32[4]{0:T(128)} %index_hbm.1, f32[4,8,256,128]{3,2,1,0:T(8,128)} %conc_hbm.1), custom_call_target="tpu_custom_call" | custom-call | flops 10485760 | bytes 4194304 | tf_op jit(solution)/shard_map/pallas_call | solution.py:476
  3.3 0.6 %collective-permute-start = (f32[8,256]{1,0:T(8,128)S(1)}, f32[8,256]{1,0:T(8,128)S(1)}, u32[]{:S(2)}, u32[]{:S(2)}) collective-permute-start(f32[8,256]{1,0:T(8,128)S(1)} %get-tuple-element.31), channel_id=1, source_target_pairs={{0,4},{4,0},{1,5},{5,1},{2,6},{6,2},{3,7},{7,3},{8,12},{12,8},{9,1... | collective-permute-start | bytes 24584 | tf_op jit(solution)/shard_map/ppermute | solution.py:445
  3.8 1.5 %shard_map.87 = (f32[4,256,8,128]{3,2,1,0:T(8,128)S(1)}, f32[4,256,8,128]{3,2,1,0:T(8,128)S(1)}, f32[2,4,8,128]{3,2,1,0:T(8,128)S(1)}) custom-call(f32[20,8,128]{2,1,0:T(8,128)S(1)} %get-tuple-element.30.plane_ref, f32[4,256,8,128]{3,2,1,0:T(8,128)S(1)} %get-tuple-element.32.conc_ref, f32[1,256,8,128]{3,2,1,0:T(8,128)S(1)} %get-tuple-element.33.early_ref, ...), custom_call_target="tpu_custom_call" | custom-call | flops 5242880 | bytes 1024 | tf_op jit(solution)/shard_map/pallas_call | solution.py:494
  5.4 1.6 %collective-permute-done.far_ref = f32[8,256]{1,0:T(8,128)S(1)} collective-permute-done((f32[8,256]{1,0:T(8,128)S(1)}, f32[8,256]{1,0:T(8,128)S(1)}, u32[]{:S(2)}, u32[]{:S(2)}) %collective-permute-start) | collective-permute-done | bytes 8224 | tf_op jit(solution)/shard_map/ppermute | solution.py:445
  7.0 0.0 collective-permute-start.3
  7.0 1.6 %collective-permute-start.1 = (f32[2,4,8,128]{3,2,1,0:T(8,128)S(1)}, f32[2,4,8,128]{3,2,1,0:T(8,128)S(1)}, u32[]{:S(2)}, u32[]{:S(2)}) collective-permute-start(f32[2,4,8,128]{3,2,1,0:T(8,128)S(1)} %get-tuple-element.37.refs_0_), channel_id=1, source_target_pairs={{0,8},{8,0},{16,24},{24,16},{1,9},{9,1},{17,25},{25,17},{2,10},{10... | collective-permute-start | bytes 98312 | tf_op jit(solution)/shard_map/ppermute | solution.py:445
  8.6 0.5 %collective-permute-start.2 = (f32[2,4,8,128]{3,2,1,0:T(8,128)S(1)}, f32[2,4,8,128]{3,2,1,0:T(8,128)S(1)}, u32[]{:S(2)}, u32[]{:S(2)}) collective-permute-start(f32[2,4,8,128]{3,2,1,0:T(8,128)S(1)} %get-tuple-element.37.refs_0_), channel_id=1, source_target_pairs={{0,16},{8,24},{16,0},{24,8},{1,17},{9,25},{17,1},{25,9},{2,18},{10... | collective-permute-start | bytes 98312 | tf_op jit(solution)/shard_map/ppermute | solution.py:445
  9.1 0.0 copy-start
  9.1 0.0 copy-start.1
  9.1 0.0 copy-start.2
  9.1 1.7 %shard_map.89 = (f32[4,256,8,128]{3,2,1,0:T(8,128)S(1)}, f32[4,256,8,128]{3,2,1,0:T(8,128)S(1)}) custom-call(f32[256,8,128]{2,1,0:T(8,128)S(1)} %get-tuple-element.38.far_ref, f32[4,256,8,128]{3,2,1,0:T(8,128)S(1)} %get-tuple-element.39.trans_ref, f32[4,256,8,128]{3,2,1,0:T(8,128)S(1)} %get-tuple-element.35.emit_ref), custom_call_target="tpu_custom_call" | custom-call | flops 5242880 | bytes 1024 | tf_op jit(solution)/shard_map/pallas_call | solution.py:508
  10.8 0.0 collective-permute-done.3.refs_3_
  10.8 0.0 collective-permute-done.1.refs_1_
  10.8 1.7 %collective-permute-done.2.refs_2_ = f32[2,4,8,128]{3,2,1,0:T(8,128)S(1)} collective-permute-done((f32[2,4,8,128]{3,2,1,0:T(8,128)S(1)}, f32[2,4,8,128]{3,2,1,0:T(8,128)S(1)}, u32[]{:S(2)}, u32[]{:S(2)}) %collective-permute-start.2) | collective-permute-done | bytes 32800 | tf_op jit(solution)/shard_map/ppermute | solution.py:445
  12.5 0.5 %collective-permute-start.4 = (f32[1,4,8,128]{3,2,1,0:T(8,128)S(1)}, f32[1,4,8,128]{3,2,1,0:T(8,128)S(1)}, u32[]{:S(2)}, u32[]{:S(2)}) collective-permute-start(f32[1,4,8,128]{3,2,1,0:T(8,128)S(1)} %get-tuple-element.43.own_ref.refs_0_), channel_id=1, source_target_pairs={{0,1},{1,0},{2,3},{3,2},{4,5},{5,4},{6,7},{7,6},{8,9},{9,8},{10,11... | collective-permute-start | bytes 49160 | tf_op jit(solution)/shard_map/ppermute | solution.py:445
  13.0 3.3 %collective-permute-done.4.refs_0_.refs_1_ = f32[1,4,8,128]{3,2,1,0:T(8,128)S(1)} collective-permute-done((f32[1,4,8,128]{3,2,1,0:T(8,128)S(1)}, f32[1,4,8,128]{3,2,1,0:T(8,128)S(1)}, u32[]{:S(2)}, u32[]{:S(2)}) %collective-permute-start.4) | collective-permute-done | bytes 16416 | tf_op jit(solution)/shard_map/ppermute | solution.py:445
  16.3 2.6 %collective-permute-start.7 = (f32[2,4,8,128]{3,2,1,0:T(8,128)S(1)}, f32[2,4,8,128]{3,2,1,0:T(8,128)S(1)}, u32[]{:S(2)}, u32[]{:S(2)}) collective-permute-start(f32[2,4,8,128]{3,2,1,0:T(8,128)S(1)} %pad_maximum_fusion), channel_id=1, source_target_pairs={{0,2},{1,3},{2,0},{3,1},{4,6},{5,7},{6,4},{7,5},{8,10},{9,11},{10,... | collective-permute-start | bytes 98312 | tf_op jit(solution)/shard_map/ppermute | solution.py:445
  18.9 0.0 collective-permute-start.5
  18.9 0.0 copy-done
  18.9 0.0 copy-done.1
  18.9 0.0 copy-done.2
  18.9 0.4 %shard_map.91 = (f32[8,24]{1,0:T(8,128)S(1)}, f32[4,8,128]{2,1,0:T(8,128)S(1)}, f32[256,32]{1,0:T(8,128)S(1)}) custom-call(s32[1,256]{1,0:T(1,128)S(1)} %bitcast.3, s32[4,256]{1,0:T(4,128)S(1)} %bitcast.2, f32[4,256,128]{2,1,0:T(8,128)S(1)} %copy-done, f32[1,4,8,128]{3,2,1,0:T(8,128)S(1)} %get-tuple-element.43.own_ref.refs_0_), custom_call_target="tpu_custom_call" | custom-call | flops 8388608 | bytes 524288 | tf_op jit(solution)/shard_map/pallas_call | solution.py:536
  19.3 3.4 %collective-permute-done.5.refs_1_ = f32[1,4,8,128]{3,2,1,0:T(8,128)S(1)} collective-permute-done((f32[1,4,8,128]{3,2,1,0:T(8,128)S(1)}, f32[1,4,8,128]{3,2,1,0:T(8,128)S(1)}, u32[]{:S(2)}, u32[]{:S(2)}) %collective-permute-start.5) | collective-permute-done | bytes 16416 | tf_op jit(solution)/shard_map/ppermute | solution.py:525
  22.7 0.1 shard_map.92
  22.8 1.7 %collective-permute-start.6 = (f32[8,256]{1,0:T(8,128)S(1)}, f32[8,256]{1,0:T(8,128)S(1)}, u32[]{:S(2)}, u32[]{:S(2)}) collective-permute-start(f32[8,256]{1,0:T(8,128)S(1)} %get-tuple-element.49), channel_id=1, source_target_pairs={{0,4},{4,0},{1,5},{5,1},{2,6},{6,2},{3,7},{7,3},{8,12},{12,8},{9,1... | collective-permute-start | bytes 24584 | tf_op jit(solution)/shard_map/ppermute | solution.py:445
  24.5 1.7 %shard_map.93 = (f32[4,256,8,128]{3,2,1,0:T(8,128)S(1)}, f32[256,8,128]{2,1,0:T(8,128)S(1)}, f32[4,8,256,128]{3,2,1,0:T(8,128)}) custom-call(f32[20,8,128]{2,1,0:T(8,128)S(1)} %get-tuple-element.30.plane_ref, f32[4,8,128]{2,1,0:T(8,128)S(1)} %get-tuple-element.51.gain_ref, f32[4,8,128]{2,1,0:T(8,128)S(1)} %get-tuple-element.52.shift_ref, ...), custom_call_target="tpu_custom_call" | custom-call | flops 10485760 | bytes 1024 | tf_op jit(solution)/shard_map/pallas_call | solution.py:553
  26.2 0.0 collective-permute-done.7.refs_2_
  26.3 0.2 collective-permute-done.6.nearer_ref
  26.5 2.2 %shard_map.95 = (f32[4,8,256,128]{3,2,1,0:T(8,128)}, f32[4,16,128]{2,1,0:T(8,128)}) custom-call(f32[20,8,128]{2,1,0:T(8,128)S(1)} %get-tuple-element.30.plane_ref, f32[8,256]{1,0:T(8,128)S(1)} %collective-permute-done.6.nearer_ref, f32[256,8,128]{2,1,0:T(8,128)S(1)} %get-tuple-element.50.near_ref, ...), custom_call_target="tpu_custom_call", output_to_operand_aliasing={{0}: (7, {}), {1}: (8, {})} | custom-call | flops 2621440 | bytes 4194304 | tf_op jit(solution)/shard_map/pallas_call | solution.py:574
  (4 shorter events, 0.1 us)
Async XLA Ops:
  3.3 3.7 %collective-permute-start = (f32[8,256]{1,0:T(8,128)S(1)}, f32[8,256]{1,0:T(8,128)S(1)}, u32[]{:S(2)}, u32[]{:S(2)}) collective-permute-start(f32[8,256]{1,0:T(8,128)S(1)} %get-tuple-element.31), channel_id=1, source_target_pairs={{0,4},{4,0},{1,5},{5,1},{2,6},{6,2},{3,7},{7,3},{8,12},{12,8},{9,1... | collective-permute-start | bytes 24584 | tf_op jit(solution)/shard_map/ppermute | solution.py:445
  7.0 3.8 %collective-permute-start.3 = (f32[2,4,8,128]{3,2,1,0:T(8,128)S(1)}, f32[2,4,8,128]{3,2,1,0:T(8,128)S(1)}, u32[]{:S(2)}, u32[]{:S(2)}) collective-permute-start(f32[2,4,8,128]{3,2,1,0:T(8,128)S(1)} %get-tuple-element.37.refs_0_), channel_id=1, source_target_pairs={{0,24},{8,16},{16,8},{24,0},{1,25},{9,17},{17,9},{25,1},{2,26},{10... | collective-permute-start | bytes 98312 | tf_op jit(solution)/shard_map/ppermute | solution.py:445
  7.0 3.8 %collective-permute-start.1 = (f32[2,4,8,128]{3,2,1,0:T(8,128)S(1)}, f32[2,4,8,128]{3,2,1,0:T(8,128)S(1)}, u32[]{:S(2)}, u32[]{:S(2)}) collective-permute-start(f32[2,4,8,128]{3,2,1,0:T(8,128)S(1)} %get-tuple-element.37.refs_0_), channel_id=1, source_target_pairs={{0,8},{8,0},{16,24},{24,16},{1,9},{9,1},{17,25},{25,17},{2,10},{10... | collective-permute-start | bytes 98312 | tf_op jit(solution)/shard_map/ppermute | solution.py:445
  8.6 3.9 %collective-permute-start.2 = (f32[2,4,8,128]{3,2,1,0:T(8,128)S(1)}, f32[2,4,8,128]{3,2,1,0:T(8,128)S(1)}, u32[]{:S(2)}, u32[]{:S(2)}) collective-permute-start(f32[2,4,8,128]{3,2,1,0:T(8,128)S(1)} %get-tuple-element.37.refs_0_), channel_id=1, source_target_pairs={{0,16},{8,24},{16,0},{24,8},{1,17},{9,25},{17,1},{25,9},{2,18},{10... | collective-permute-start | bytes 98312 | tf_op jit(solution)/shard_map/ppermute | solution.py:445
  9.1 9.8 %copy-start = (f32[4,256,128]{2,1,0:T(8,128)S(1)}, f32[4,256,128]{2,1,0:T(8,128)}, u32[]{:S(2)}) copy-start(f32[4,256,128]{2,1,0:T(8,128)} %measured_ref.5) | copy-start | bytes 1572868
  9.1 9.8 %copy-start.1 = (s32[256,4]{0,1:T(4,128)S(1)}, s32[256,4]{0,1:T(4,128)}, u32[]{:S(2)}) copy-start(s32[256,4]{0,1:T(4,128)} %param.12) | copy-start | bytes 12292
  9.1 9.8 %copy-start.2 = (s32[256]{0:T(256)S(1)}, s32[256]{0:T(256)}, u32[]{:S(2)}) copy-start(s32[256]{0:T(256)} %param.11) | copy-start | bytes 3076
  12.5 3.8 %collective-permute-start.4 = (f32[1,4,8,128]{3,2,1,0:T(8,128)S(1)}, f32[1,4,8,128]{3,2,1,0:T(8,128)S(1)}, u32[]{:S(2)}, u32[]{:S(2)}) collective-permute-start(f32[1,4,8,128]{3,2,1,0:T(8,128)S(1)} %get-tuple-element.43.own_ref.refs_0_), channel_id=1, source_target_pairs={{0,1},{1,0},{2,3},{3,2},{4,5},{5,4},{6,7},{7,6},{8,9},{9,8},{10,11... | collective-permute-start | bytes 49160 | tf_op jit(solution)/shard_map/ppermute | solution.py:445
  16.3 9.9 %collective-permute-start.7 = (f32[2,4,8,128]{3,2,1,0:T(8,128)S(1)}, f32[2,4,8,128]{3,2,1,0:T(8,128)S(1)}, u32[]{:S(2)}, u32[]{:S(2)}) collective-permute-start(f32[2,4,8,128]{3,2,1,0:T(8,128)S(1)} %pad_maximum_fusion), channel_id=1, source_target_pairs={{0,2},{1,3},{2,0},{3,1},{4,6},{5,7},{6,4},{7,5},{8,10},{9,11},{10,... | collective-permute-start | bytes 98312 | tf_op jit(solution)/shard_map/ppermute | solution.py:445
  18.9 3.7 %collective-permute-start.5 = (f32[1,4,8,128]{3,2,1,0:T(8,128)S(1)}, f32[1,4,8,128]{3,2,1,0:T(8,128)S(1)}, u32[]{:S(2)}, u32[]{:S(2)}) collective-permute-start(f32[1,4,8,128]{3,2,1,0:T(8,128)S(1)} %get-tuple-element.43.own_ref.refs_0_), channel_id=1, source_target_pairs={{0,8},{1,2},{2,1},{3,11},{8,0},{9,10},{10,9},{11,3},{16,24},{17,18... | collective-permute-start | bytes 49160 | tf_op jit(solution)/shard_map/ppermute | solution.py:525
  22.8 3.7 %collective-permute-start.6 = (f32[8,256]{1,0:T(8,128)S(1)}, f32[8,256]{1,0:T(8,128)S(1)}, u32[]{:S(2)}, u32[]{:S(2)}) collective-permute-start(f32[8,256]{1,0:T(8,128)S(1)} %get-tuple-element.49), channel_id=1, source_target_pairs={{0,4},{4,0},{1,5},{5,1},{2,6},{6,2},{3,7},{7,3},{8,12},{12,8},{9,1... | collective-permute-start | bytes 24584 | tf_op jit(solution)/shard_map/ppermute | solution.py:445
